TPU v7x, 32 devices: a whole 2x2x4 slice. The times are simulated.
32 devices in a mesh: feat: 8 (over z, y), ex: 4 (over x, core).
Axes of the slice: x: 2, y: 2, z: 4, core: 2. Of those that a mesh axis runs over, the one named last changes fastest.
Arguments:
- examples: bfloat16 [4096, 262144], P('ex', 'feat'), may hold values from -6 to 6
- weights: bfloat16 [262144], P('feat'), may hold values from -0.01171875 to 0.01171875
- labels: int32 [4096], P('ex'), may hold values from 0 to 1
- split: int32 [4096], P('ex'), may hold values 0 or 1
- val_weight: float32 [32, 4096], P(None, 'ex'), may hold values from 0.1 to 10
- strengths: float32 [256], replicated, may hold values from 0.05 to 1
- block_ids: int32 [262144], P('feat'), may hold values from 0 to 255
Outputs:
- solve: float32 [32, 262144], P(None, ('feat', 'ex'))
- hypergrad: float32 [32, 256], P(None, ('feat', 'ex'))
All inputs are finite; a program needn't handle non-finite values. No bound on the sum of `split` on one device may be relied on, other than what follows from the above.
Results may differ from a plain program's by a relative error of at most 0.0029.
Values may be sent and summed in bfloat16 or wider, within the bound.
A program may use at most 128 MiB of HBM per device.

v0:
```python
import jax
import jax.numpy as jnp
from jax import lax
from jax.sharding import PartitionSpec as P


def shards(examples, weights, labels, split, val_weight, strengths, block_ids):
    n_ex = lax.axis_size("ex")
    n_feat = lax.axis_size("feat")
    ex_pos = lax.axis_index("ex")
    feat_pos = lax.axis_index("feat")
    total = examples.shape[0] * n_ex
    width = examples.shape[1]
    share = width // n_ex
    blocks = strengths.shape[0]
    nb_local = blocks // (n_feat * n_ex)
    margin = lax.psum(jnp.dot(examples, weights, preferred_element_type=jnp.float32), "feat")
    prob = 1.0 / (1.0 + jnp.exp(-margin))
    train = split.astype(jnp.float32)
    curvew = train * prob * (1.0 - prob)
    err = (1.0 - train) * (prob - labels.astype(jnp.float32))
    gradw = (val_weight * err[None, :] / jnp.sqrt(jnp.float32(total))).astype(jnp.bfloat16)
    grad_part = jnp.dot(gradw, examples, preferred_element_type=jnp.float32)
    onehot = (block_ids[:, None] == jnp.arange(blocks, dtype=jnp.int32)[None, :]).astype(
        jnp.float32
    )
    lamf = jnp.dot(onehot, strengths, precision=lax.Precision.HIGHEST)
    wfloat = weights.astype(jnp.float32)
    start = ex_pos * share
    rhs = lax.psum_scatter(grad_part, "ex", scatter_dimension=1, tiled=True)
    lam_loc = lax.dynamic_slice_in_dim(lamf, start, share, 0)
    onehot_loc = lax.dynamic_slice_in_dim(onehot, start, share, 0)
    w_loc = lax.dynamic_slice_in_dim(wfloat, start, share, 0)

    def norm_sum(vec):
        return lax.psum(jnp.sum(vec * vec, axis=1), ("feat", "ex"))

    solve = jnp.zeros_like(rhs)
    resid = rhs
    direc = rhs
    norm_now = norm_sum(resid)
    for step in range(2):
        full_dir = lax.all_gather(direc.astype(jnp.bfloat16), "ex", axis=1, tiled=True)
        tang = lax.dot_general(
            full_dir, examples, (((1,), (1,)), ((), ())), preferred_element_type=jnp.float32
        )
        tang = lax.psum(tang, "feat")
        wtang = (curvew[None, :] * tang).astype(jnp.bfloat16)
        prod = lax.psum_scatter(
            jnp.dot(wtang, examples, preferred_element_type=jnp.float32),
            "ex",
            scatter_dimension=1,
            tiled=True,
        )
        image = prod / jnp.float32(total) + lam_loc[None, :] * direc
        alpha = norm_now / lax.psum(jnp.sum(direc * image, axis=1), ("feat", "ex"))
        solve = solve + alpha[:, None] * direc
        resid = resid - alpha[:, None] * image
        if step == 0:
            norm_next = norm_sum(resid)
            direc = resid + (norm_next / norm_now)[:, None] * direc
            norm_now = norm_next
    partial_blocks = jnp.dot(solve * w_loc[None, :], onehot_loc, precision=lax.Precision.HIGHEST)
    block_sums = lax.psum_scatter(partial_blocks, ("feat", "ex"), scatter_dimension=1, tiled=True)
    own = lax.dynamic_slice_in_dim(strengths, (feat_pos * n_ex + ex_pos) * nb_local, nb_local, 0)
    return (solve, -own[None, :] * block_sums)


def solution(mesh):
    placed = (P("ex", "feat"), P("feat"), P("ex"), P("ex"), P(None, "ex"), P(), P("feat"))
    return jax.shard_map(
        shards,
        mesh=mesh,
        in_specs=placed,
        out_specs=(P(None, ("feat", "ex")), P(None, ("feat", "ex"))),
        check_vma=False,
    )
```

profile of v0, /device:TPU:0, one launch (start us, length us, event | category | flops | bytes accessed | tf_op | source)
XLA Modules:
  0.0 695.1 jit_solution(9688805539957404620)
XLA Ops:
  7.2 0.0 reduce-scatter.4.cloned.1.call-start
  7.2 0.9 reshape.14
  8.1 0.0 copy-start.5
  8.1 0.0 copy-start.6
  8.1 0.0 copy-start.3
  8.2 26.6 %fusion.15 = f32[1,1024]{1,0:T(1,128)S(1)} fusion(bf16[1024,32768]{1,0:T(8,128)(2,1)} %param.7, bf16[32768,1]{0,1:T(2,128)(2,1)S(1)} %reshape.14), kind=kOutput, calls=%fused_computation.33 | convolution fusion | flops 67108864 | bytes 67178496 | tf_op jit(solution)/shard_map/dot_general | solution.py:17
  34.8 23.2 %psum.49 = f32[1024]{0:T(1024)S(1)} all-reduce(f32[1024]{0:T(1024)S(1)} %bitcast.13), channel_id=1, replica_groups=mesh['feat'=8,'ex'=4] {'feat'}, use_global_device_ids=true, to_apply=%region_0.0 | all-reduce | flops 1024 | bytes 8192 | tf_op jit(solution)/shard_map/psum | solution.py:17
  58.0 0.0 copy-done.5
  58.0 0.0 copy-done.6
  58.0 0.0 copy-done.3
  58.0 25.3 %fusion.5 = f32[32,32768]{1,0:T(8,128)} fusion(bf16[1024,32768]{1,0:T(8,128)(2,1)} %param.7, f32[32,1024]{1,0:T(8,128)S(1)} %copy-done.3, f32[1024]{0:T(1024)S(1)} %get-tuple-element.7), kind=kOutput, calls=%fused_computation.17 | convolution fusion | flops 2147581952 | bytes 71438336 | tf_op jit(solution)/shard_map/dot_general | solution.py:23
  83.3 0.0 reduce-scatter.4.cloned.1.call-update
  83.3 0.0 all-gather.3.cloned.1.call-start
  83.3 41.8 %reduce-scatter.4.cloned.1.call-done = f32[32,8192]{1,0:T(8,128)} async-done(((f32[32,32768]{1,0:T(8,128)}), f32[32,8192]{1,0:T(8,128)}) %reduce-scatter.4.cloned.1.call-update) | async-done | bytes 1048592 | tf_op jit(solution)/shard_map/reduce_scatter | solution.py:30
  125.2 2.1 convert_element_type.28
  127.2 0.0 all-gather.3.cloned.1.call-update
  127.2 0.0 all-reduce.5.cloned.1.call-start
  127.3 22.7 %all-gather.3.cloned.1.call-done = bf16[32,32768]{1,0:T(8,128)(2,1)} async-done(((bf16[32,8192]{1,0:T(8,128)(2,1)}), bf16[32,32768]{1,0:T(8,128)(2,1)}) %all-gather.3.cloned.1.call-update) | async-done | bytes 2097168 | tf_op jit(solution)/shard_map/all_gather | solution.py:43
  150.0 27.6 %fusion.16 = f32[32,1024]{1,0:T(8,128)} fusion(bf16[32,32768]{1,0:T(8,128)(2,1)} %all-gather.3.cloned.1.call-done, bf16[1024,32768]{1,0:T(8,128)(2,1)} %param.7), kind=kOutput, calls=%fused_computation.34 | convolution fusion | flops 2147483648 | bytes 69337088 | tf_op jit(solution)/shard_map/dot_general | solution.py:44
  177.6 0.0 all-reduce.5.cloned.1.call-update
  177.6 0.0 reduce-scatter.6.cloned.1.call-start
  177.7 70.5 %all-reduce.5.cloned.1.call-done = f32[32,1024]{1,0:T(8,128)} async-done(((f32[32,1024]{1,0:T(8,128)}), f32[32,1024]{1,0:T(8,128)}) %all-reduce.5.cloned.1.call-update) | async-done | bytes 131088 | tf_op jit(solution)/shard_map/psum | solution.py:47
  248.2 0.0 copy-start.4
  248.2 0.0 copy-start.7
  248.2 26.5 %fusion.6 = f32[32,32768]{1,0:T(8,128)} fusion(bf16[1024,32768]{1,0:T(8,128)(2,1)} %param.7, f32[32,1024]{1,0:T(8,128)} %all-reduce.5.cloned.1.call-done, f32[1024]{0:T(1024)S(1)} %get-tuple-element.6), kind=kOutput, calls=%fused_computation.18 | convolution fusion | flops 2147549184 | bytes 71438336 | tf_op jit(solution)/shard_map/dot_general | solution.py:50
  274.6 0.0 copy-start
  274.6 0.0 reduce-scatter.6.cloned.1.call-update
  274.7 0.0 all-gather.5.cloned.1.call-start
  274.7 0.0 copy-done.4
  274.7 0.0 copy-done.7
  274.7 17.1 %fusion.3 = f32[1,32768]{1,0:T(1,128)S(1)} fusion(f32[256,1]{0,1:T(1,128)S(1)} %bitcast.15, s32[32768]{0:T(1024)S(1)} %copy-done.4), kind=kOutput, calls=%fused_computation.12 | convolution fusion | flops 109051904 | bytes 263168 | tf_op jit(solution)/shard_map/dot_general | solution.py:27
  291.8 26.6 %reduce-scatter.6.cloned.1.call-done = f32[32,8192]{1,0:T(8,128)} async-done(((f32[32,32768]{1,0:T(8,128)}), f32[32,8192]{1,0:T(8,128)}) %reduce-scatter.6.cloned.1.call-update) | async-done | bytes 1048592 | tf_op jit(solution)/shard_map/reduce_scatter | solution.py:49
  318.4 0.0 copy-done
  318.4 1.6 multiply_reduce_fusion.2
  320.0 39.3 %all-reduce.1 = (f32[32]{0:T(128)S(1)}, f32[32]{0:T(128)S(1)}) all-reduce(f32[32]{0:T(128)S(1)} %get-tuple-element.3, f32[32]{0:T(128)S(1)} %get-tuple-element.2), channel_id=1, replica_groups=mesh['feat'=8,'ex'=4] {'feat','ex'}, use_global_device_ids=true, to_apply=%region_3.0 | all-reduce | flops 64 | bytes 512 | tf_op jit(solution)/shard_map/psum | solution.py:36
  359.3 1.6 multiply_reduce_fusion.1
  360.9 41.1 %psum.53 = f32[32]{0:T(128)S(1)} all-reduce(f32[32]{0:T(128)S(1)} %multiply_reduce_fusion.1), channel_id=1, replica_groups=mesh['feat'=8,'ex'=4] {'feat','ex'}, use_global_device_ids=true, to_apply=%region_9.0 | all-reduce | flops 32 | bytes 256 | tf_op jit(solution)/shard_map/psum | solution.py:36
  402.0 2.3 fusion.14
  404.3 0.0 all-gather.5.cloned.1.call-update
  404.3 0.0 all-reduce.7.cloned.1.call-start
  404.4 22.5 %all-gather.5.cloned.1.call-done = bf16[32,32768]{1,0:T(8,128)(2,1)} async-done(((bf16[32,8192]{1,0:T(8,128)(2,1)}), bf16[32,32768]{1,0:T(8,128)(2,1)}) %all-gather.5.cloned.1.call-update) | async-done | bytes 2097168 | tf_op jit(solution)/shard_map/all_gather | solution.py:43
  426.8 27.6 %fusion.17 = f32[32,1024]{1,0:T(8,128)} fusion(bf16[32,32768]{1,0:T(8,128)(2,1)} %all-gather.5.cloned.1.call-done, bf16[1024,32768]{1,0:T(8,128)(2,1)} %param.7), kind=kOutput, calls=%fused_computation.35 | convolution fusion | flops 2147483648 | bytes 69337088 | tf_op jit(solution)/shard_map/dot_general | solution.py:44
  454.5 0.0 all-reduce.7.cloned.1.call-update
  454.5 0.0 reduce-scatter.8.cloned.1.call-start
  454.5 70.5 %all-reduce.7.cloned.1.call-done = f32[32,1024]{1,0:T(8,128)} async-done(((f32[32,1024]{1,0:T(8,128)}), f32[32,1024]{1,0:T(8,128)}) %all-reduce.7.cloned.1.call-update) | async-done | bytes 131088 | tf_op jit(solution)/shard_map/psum | solution.py:47
  525.0 26.4 %fusion.7 = f32[32,32768]{1,0:T(8,128)} fusion(bf16[1024,32768]{1,0:T(8,128)(2,1)} %param.7, f32[32,1024]{1,0:T(8,128)} %all-reduce.7.cloned.1.call-done, f32[1024]{0:T(1024)S(1)} %get-tuple-element.6), kind=kOutput, calls=%fused_computation.19 | convolution fusion | flops 2147549184 | bytes 71438336 | tf_op jit(solution)/shard_map/dot_general | solution.py:50
  551.5 0.0 copy-start.1
  551.5 0.0 reduce-scatter.8.cloned.1.call-update
  551.5 0.1 dynamic-slice_negate_fusion
  551.6 0.8 dynamic-slice_convert_fusion
  552.4 15.8 %iota_compare_fusion = pred[32768,256]{1,0:T(32,128)(4,1)} fusion(s32[32768]{0:T(1024)S(1)} %copy-done.4), kind=kLoop, calls=%fused_computation | loop fusion | flops 8388608 | bytes 8519680 | tf_op jit(solution)/shard_map/eq | solution.py:24
  568.2 27.0 %reduce-scatter.8.cloned.1.call-done = f32[32,8192]{1,0:T(8,128)} async-done(((f32[32,32768]{1,0:T(8,128)}), f32[32,8192]{1,0:T(8,128)}) %reduce-scatter.8.cloned.1.call-update) | async-done | bytes 1048592 | tf_op jit(solution)/shard_map/reduce_scatter | solution.py:49
  595.2 0.0 copy-done.1
  595.2 1.8 multiply_reduce_fusion
  597.0 39.5 %psum.55 = f32[32]{0:T(128)S(1)} all-reduce(f32[32]{0:T(128)S(1)} %multiply_reduce_fusion), channel_id=1, replica_groups=mesh['feat'=8,'ex'=4] {'feat','ex'}, use_global_device_ids=true, to_apply=%region_13.0 | all-reduce | flops 32 | bytes 256 | tf_op jit(solution)/shard_map/psum | solution.py:56
  636.5 0.4 multiply_add_fusion
  636.9 0.0 copy-start.2
  637.0 8.6 %fusion = f32[32,256]{0,1:T(8,128)S(1)} fusion(pred[32768,256]{1,0:T(32,128)(4,1)} %iota_compare_fusion, s32[]{:T(128)S(6)} %select_n.8, f32[32,8192]{1,0:T(8,128)S(1)} %multiply_add_fusion, f32[8192]{0:T(1024)S(1)} %dynamic-slice_convert_fusion), kind=kOutput, calls=%fused_computation.1 | convolution fusion | flops 805568512 | bytes 3211268 | tf_op jit(solution)/shard_map/dot_general | solution.py:63
  645.6 42.0 %all-reduce = f32[32,256]{0,1:T(8,128)S(1)} all-reduce(f32[32,256]{0,1:T(8,128)S(1)} %fusion), channel_id=5, replica_groups=mesh['feat'=8,'ex'=4] {'feat','ex'}, use_global_device_ids=true, to_apply=%region_14.0.clone | all-reduce | flops 8192 | bytes 65536
  687.6 0.7 dynamic-slice_multiply_fusion
  688.3 0.0 copy-done.2
  (5 shorter events, 0.0 us)
Async XLA Ops:
  7.2 118.0 %reduce-scatter.4.cloned.1.call-start = ((), (), s32[]{:S(2)}) async-start(), calls=%async_computation.3 | async-start | bytes 5242880 | tf_op jit(solution)/shard_map/reduce_scatter | solution.py:30
  8.1 49.8 %copy-start.5 = (s32[1024]{0:T(1024)S(1)}, s32[1024]{0:T(1024)}, u32[]{:S(2)}) copy-start(s32[1024]{0:T(1024)} %param.10) | copy-start | bytes 12292
  8.1 49.8 %copy-start.6 = (s32[1024]{0:T(1024)S(1)}, s32[1024]{0:T(1024)}, u32[]{:S(2)}) copy-start(s32[1024]{0:T(1024)} %param.9) | copy-start | bytes 12292
  8.1 49.8 %copy-start.3 = (f32[32,1024]{1,0:T(8,128)S(1)}, f32[32,1024]{1,0:T(8,128)}, u32[]{:S(2)}) copy-start(f32[32,1024]{1,0:T(8,128)} %param.11) | copy-start | bytes 393220
  83.3 66.7 %all-gather.3.cloned.1.call-start = ((), (), s32[]{:S(2)}) async-start(), calls=%async_computation.4 | async-start | bytes 2621440 | tf_op jit(solution)/shard_map/all_gather | solution.py:43
  127.2 120.9 %all-reduce.5.cloned.1.call-start = ((), (), s32[]{:S(2)}) async-start(), calls=%async_computation.5 | async-start | bytes 262144 | tf_op jit(solution)/shard_map/psum | solution.py:47
  177.6 140.8 %reduce-scatter.6.cloned.1.call-start = ((), (), s32[]{:S(2)}) async-start(), calls=%async_computation.6 | async-start | bytes 5242880 | tf_op jit(solution)/shard_map/reduce_scatter | solution.py:49
  248.2 26.5 %copy-start.4 = (s32[32768]{0:T(1024)S(1)}, s32[32768]{0:T(1024)}, u32[]{:S(2)}) copy-start(s32[32768]{0:T(1024)} %param.13) | copy-start | bytes 393220
  248.2 26.6 %copy-start.7 = (f32[256]{0:T(256)S(1)}, f32[256]{0:T(256)}, u32[]{:S(2)}) copy-start(f32[256]{0:T(256)} %param.12) | copy-start | bytes 3076
  274.6 43.8 %copy-start = (f32[32,8192]{1,0:T(8,128)S(1)}, f32[32,8192]{1,0:T(8,128)}, u32[]{:S(2)}) copy-start(f32[32,8192]{1,0:T(8,128)} %reduce-scatter.4.cloned.1.call-done) | copy-start | bytes 3145732
  274.7 152.2 %all-gather.5.cloned.1.call-start = ((), (), s32[]{:S(2)}) async-start(), calls=%async_computation.7 | async-start | bytes 2621440 | tf_op jit(solution)/shard_map/all_gather | solution.py:43
  404.3 120.7 %all-reduce.7.cloned.1.call-start = ((), (), s32[]{:S(2)}) async-start(), calls=%async_computation.8 | async-start | bytes 262144 | tf_op jit(solution)/shard_map/psum | solution.py:47
  454.5 140.7 %reduce-scatter.8.cloned.1.call-start = ((), (), s32[]{:S(2)}) async-start(), calls=%async_computation.9 | async-start | bytes 5242880 | tf_op jit(solution)/shard_map/reduce_scatter | solution.py:49
  551.5 43.7 %copy-start.1 = (f32[32,8192]{1,0:T(8,128)S(1)}, f32[32,8192]{1,0:T(8,128)}, u32[]{:S(2)}) copy-start(f32[32,8192]{1,0:T(8,128)} %reduce-scatter.6.cloned.1.call-done) | copy-start | bytes 3145732
  636.9 51.3 %copy-start.2 = (f32[32,8192]{1,0:T(8,128)}, f32[32,8192]{1,0:T(8,128)S(1)}, u32[]{:S(2)}) copy-start(f32[32,8192]{1,0:T(8,128)S(1)} %multiply_add_fusion) | copy-start | bytes 3145732
Sparse Core Ops, SparseCore 0:
  83.4 41.7 reduce-scatter.3
  127.4 22.5 all-gather.2
  177.7 70.3 all-reduce.4
  274.8 43.5 reduce-scatter.5
  404.4 22.3 all-gather.4
  454.6 70.3 all-reduce.6
  551.6 43.5 reduce-scatter.7
where the time goes:
time: 696 us; the launch traced here: 695 us
  waiting for transfers between devices  282 us (41%)
  matrix products  186 us (27%)
  blocking collectives  185 us (27%)
  other arithmetic  27.1 us (4%)
  between operations  14.3 us (2%)
    psum x2, waiting for transfers between devices, shards(): tang = lax.psum(tang, 'feat')  141 us
    psum x2, blocking collectives, norm_sum(): return lax.psum(jnp.sum(vec * vec, axis=1), ('feat', 'ex'))  80.4 us
    dot_general x2, matrix products, shards(): lax.dot_general(full_dir, examples, (((1,), (1,)), ((), ())), preferred_e...  55.3 us
    reduce_scatter x2, waiting for transfers between devices, shards(): lax.psum_scatter(jnp.dot(wtang, examples, preferred_element_type=jnp.floa...  53.6 us
    dot_general x2, matrix products, shards(): jnp.dot(wtang, examples, preferred_element_type=jnp.float32)  52.9 us
    all_gather x2, waiting for transfers between devices, shards(): lax.all_gather(direc.astype(jnp.bfloat16), 'ex', axis=1, tiled=True)  45.1 us
    unnamed x1, blocking collectives  42 us
    reduce_scatter x1, waiting for transfers between devices, shards(): rhs = lax.psum_scatter(grad_part, 'ex', scatter_dimension=1, tiled=True)  41.8 us
  transfers between devices with their start and end apart: 7, of which 7 were waited for; matrix products, arithmetic and copies ran while one was open for 5% of the time, Pallas kernels for 0%

commit v1 on v0

v1 whole, which is shorter than its diff:
```python
import functools

import jax
import jax.numpy as jnp
from jax import lax
from jax.experimental import pallas as pl
from jax.experimental.pallas import tpu as pltpu
from jax.sharding import PartitionSpec as P

MESH = pl.DeviceIdType.MESH
VMEM = pl.BlockSpec(memory_space=pltpu.VMEM)
LANES = 128


def address(axis, pos):
    if axis == "feat":
        return (pos, lax.axis_index("ex"))
    return (lax.axis_index("feat"), pos)


def flip(pos, offset):
    out, mask = pos, 1
    while mask <= offset:
        if offset & mask:
            out = out + mask * (1 - 2 * lax.rem(lax.div(pos, mask), 2))
        mask *= 2
    return out


def meet(axis, peers):
    barrier = pltpu.get_barrier_semaphore()
    for peer in peers:
        pl.semaphore_signal(barrier, inc=1, device_id=address(axis, peer), device_id_type=MESH)
    pl.semaphore_wait(barrier, len(peers))


def total_kernel(axis, n, x_ref, out_ref, slots, send_sem, recv_sem):
    me = lax.axis_index(axis)
    peers = [lax.rem(me + k, n) for k in range(1, n)]
    meet(axis, peers)
    copies = []
    for k, peer in enumerate(peers):
        copy = pltpu.make_async_remote_copy(
            src_ref=x_ref,
            dst_ref=slots.at[k],
            send_sem=send_sem.at[k],
            recv_sem=recv_sem.at[k],
            device_id=address(axis, peer),
            device_id_type=MESH,
        )
        copy.start()
        copies.append(copy)
    total = x_ref[...]
    for k, copy in enumerate(copies):
        copy.wait_recv()
        total = total + slots[k]
    out_ref[...] = total
    for copy in copies:
        copy.wait_send()


def small_total(x, axis, ident):
    n = lax.axis_size(axis)
    if n == 1:
        return x
    return pl.pallas_call(
        functools.partial(total_kernel, axis, n),
        out_shape=jax.ShapeDtypeStruct(x.shape, x.dtype),
        in_specs=[VMEM],
        out_specs=VMEM,
        scratch_shapes=[
            pltpu.VMEM((n - 1,) + x.shape, x.dtype),
            pltpu.SemaphoreType.DMA((n - 1,)),
            pltpu.SemaphoreType.DMA((n - 1,)),
        ],
        compiler_params=pltpu.CompilerParams(collective_id=ident, has_side_effects=True),
    )(x)


def reduce_kernel(axis, n, x_ref, out_ref, slots, full, send_sem, recv_sem):
    me = lax.axis_index(axis)
    peers = [lax.rem(me + k, n) for k in range(1, n)]
    meet(axis, peers)
    first, second = [], []
    for k, peer in enumerate(peers):
        copy = pltpu.make_async_remote_copy(
            src_ref=x_ref.at[peer],
            dst_ref=slots.at[k],
            send_sem=send_sem.at[0, k],
            recv_sem=recv_sem.at[0, k],
            device_id=address(axis, peer),
            device_id_type=MESH,
        )
        copy.start()
        first.append(copy)
    total = x_ref[me]
    for k, copy in enumerate(first):
        copy.wait_recv()
        total = total + slots[k]
    full[me] = total
    for k, peer in enumerate(peers):
        copy = pltpu.make_async_remote_copy(
            src_ref=full.at[me],
            dst_ref=full.at[me],
            send_sem=send_sem.at[1, k],
            recv_sem=recv_sem.at[1, k],
            device_id=address(axis, peer),
            device_id_type=MESH,
        )
        copy.start()
        second.append(copy)
    for copy in second:
        copy.wait_recv()
    out_ref[...] = full[...]
    for copy in first + second:
        copy.wait_send()


def large_total(x, axis, ident):
    n = lax.axis_size(axis)
    if n == 1:
        return x
    rows = x.shape[0]
    y = x.reshape(n, rows // n, LANES)
    out = pl.pallas_call(
        functools.partial(reduce_kernel, axis, n),
        out_shape=jax.ShapeDtypeStruct(y.shape, y.dtype),
        in_specs=[VMEM],
        out_specs=VMEM,
        scratch_shapes=[
            pltpu.VMEM((n - 1,) + y.shape[1:], y.dtype),
            pltpu.VMEM(y.shape, y.dtype),
            pltpu.SemaphoreType.DMA((2, n - 1)),
            pltpu.SemaphoreType.DMA((2, n - 1)),
        ],
        compiler_params=pltpu.CompilerParams(collective_id=ident, has_side_effects=True),
    )(y)
    return out.reshape(rows, LANES)


def spread_kernel(n, share, based, *refs):
    if based:
        x_ref, base_ref, coef_ref, own_ref, all_ref = refs[:5]
    else:
        x_ref, own_ref, all_ref = refs[:3]
    acc, outbox, inbox, full, out_sem, in_sem, send_sem, recv_sem = refs[-8:]
    me = lax.axis_index("ex")
    masks = []
    while 2 ** len(masks) < n:
        masks.append(2 ** len(masks))
    meet("ex", [flip(me, mask) for mask in masks])

    copies = []
    slot = 0
    for level, mask in enumerate(masks):
        low = lax.rem(me, mask)
        bit = lax.rem(lax.div(me, mask), 2)
        groups = n // (2 * mask)
        upper = lax.div(me, 2 * mask)
        sent = []
        for k in range(groups):
            group = lax.rem(upper + 1 + k, groups) if groups > 1 else 0
            away = group * 2 * mask + (1 - bit) * mask + low
            kept = group * 2 * mask + bit * mask + low
            if level == 0:
                part = x_ref[:, pl.ds(pl.multiple_of(away * share, share), share)]
            else:
                part = acc[away]
            outbox[slot] = part.astype(jnp.bfloat16)
            copy = pltpu.make_async_remote_copy(
                src_ref=outbox.at[slot],
                dst_ref=inbox.at[slot],
                send_sem=out_sem.at[slot],
                recv_sem=in_sem.at[slot],
                device_id=address("ex", flip(me, mask)),
                device_id_type=MESH,
            )
            copy.start()
            sent.append((copy, kept, slot))
            slot += 1
        nexts = []
        for copy, kept, at in sent:
            if level == 0:
                mine = x_ref[:, pl.ds(pl.multiple_of(kept * share, share), share)]
            else:
                mine = acc[kept]
            nexts.append((copy, kept, at, mine))
        for copy, kept, at, mine in nexts:
            copy.wait_recv()
            acc[kept] = mine + inbox[at].astype(jnp.float32)
            copies.append(copy)
    own = acc[me] if n > 1 else x_ref[...]
    if based:
        own = base_ref[...] + coef_ref[:, 0:1] * own
    own_ref[...] = own
    full[me] = own.astype(jnp.bfloat16)

    ident = {}
    held = [0]
    order = []
    for mask in reversed(masks):
        for offset in held:
            ident[mask, offset] = len(ident)
        order.append((mask, list(held)))
        held = held + [mask ^ offset for offset in held]

    def passing(mask, offset):
        at = ident[mask, offset]
        chunk = flip(me, offset)
        return pltpu.make_async_remote_copy(
            src_ref=full.at[chunk],
            dst_ref=full.at[chunk],
            send_sem=send_sem.at[at],
            recv_sem=recv_sem.at[at],
            device_id=address("ex", flip(me, mask)),
            device_id_type=MESH,
        )

    live = {}
    for mask in reversed(masks):
        live[mask, 0] = passing(mask, 0)
        live[mask, 0].start()
    all_ref[:, pl.ds(pl.multiple_of(me * share, share), share)] = full[me]
    for mask, offsets in order:
        for offset in offsets:
            live[mask, offset].wait_recv()
            arrived = mask ^ offset
            for smaller in reversed(masks):
                if smaller < mask:
                    live[smaller, arrived] = passing(smaller, arrived)
                    live[smaller, arrived].start()
            chunk = flip(me, arrived)
            all_ref[:, pl.ds(pl.multiple_of(chunk * share, share), share)] = full[chunk]
    for copy in copies:
        copy.wait_send()
    for copy in live.values():
        copy.wait_send()


def spread(x, base, coef, ident):
    n = lax.axis_size("ex")
    rows, width = x.shape
    share = width // n
    based = base is not None
    count = max(n - 1, 1)
    return pl.pallas_call(
        functools.partial(spread_kernel, n, share, based),
        out_shape=(
            jax.ShapeDtypeStruct((rows, share), jnp.float32),
            jax.ShapeDtypeStruct((rows, width), jnp.bfloat16),
        ),
        in_specs=[VMEM] * (3 if based else 1),
        out_specs=(VMEM, VMEM),
        scratch_shapes=[
            pltpu.VMEM((n, rows, share), jnp.float32),
            pltpu.VMEM((count, rows, share), jnp.bfloat16),
            pltpu.VMEM((count, rows, share), jnp.bfloat16),
            pltpu.VMEM((n, rows, share), jnp.bfloat16),
        ]
        + [pltpu.SemaphoreType.DMA((count,))] * 4,
        compiler_params=pltpu.CompilerParams(collective_id=ident, has_side_effects=True),
    )(*((x, base, coef) if based else (x,)))


def to_rows(x):
    rows, cols = x.shape
    if cols % LANES == 0:
        return x.reshape(rows, cols // LANES, LANES).transpose(1, 0, 2).reshape(-1, LANES)
    flat = x.reshape(-1)
    return jnp.pad(flat, (0, -flat.shape[0] % LANES)).reshape(-1, LANES)


def from_rows(x, shape):
    rows, cols = shape
    if cols % LANES == 0:
        return x.reshape(cols // LANES, rows, LANES).transpose(1, 0, 2).reshape(rows, cols)
    return x.reshape(-1)[: rows * cols].reshape(rows, cols)


def pack(arrays, multiple):
    out = jnp.concatenate([to_rows(x) for x in arrays], axis=0)
    return jnp.pad(out, ((0, -out.shape[0] % multiple), (0, 0)))


def unpack(x, arrays):
    out, at = [], 0
    for like in arrays:
        count = -(-like.shape[0] * like.shape[1] // LANES)
        out.append(from_rows(x[at : at + count], like.shape))
        at += count
    return out


def shards(examples, weights, labels, split, val_weight, strengths, block_ids):
    n_ex = lax.axis_size("ex")
    n_feat = lax.axis_size("feat")
    ex_pos = lax.axis_index("ex")
    feat_pos = lax.axis_index("feat")
    total = examples.shape[0] * n_ex
    width = examples.shape[1]
    share = width // n_ex
    blocks = strengths.shape[0]
    nb_feat = blocks // n_feat
    nb_local = nb_feat // n_ex
    start = ex_pos * share

    def reduced(x, pieces):
        parts = []
        for _ in range(pieces):
            part = lax.reduce_precision(x, 8, 7)
            parts.append(part.astype(jnp.bfloat16))
            x = x - part
        return parts

    part = jnp.dot(examples, weights, preferred_element_type=jnp.float32)
    (margin,) = unpack(small_total(pack([part[None, :]], 8), "feat", 0), [part[None, :]])
    margin = margin[0]
    prob = 1.0 / (1.0 + jnp.exp(-margin))
    train = split.astype(jnp.float32)
    curvew = train * prob * (1.0 - prob)
    err = (1.0 - train) * (prob - labels.astype(jnp.float32))
    gradw = (val_weight * err[None, :] / jnp.sqrt(jnp.float32(total))).astype(jnp.bfloat16)
    rhs, low = spread(jnp.dot(gradw, examples, preferred_element_type=jnp.float32), None, None, 1)

    ids_loc = lax.dynamic_slice_in_dim(block_ids, start, share, 0)
    w_loc = lax.dynamic_slice_in_dim(weights, start, share, 0).astype(jnp.float32)
    onehot = (ids_loc[:, None] == jnp.arange(blocks, dtype=jnp.int32)[None, :]).astype(jnp.bfloat16)
    levels = jnp.stack(reduced(strengths, 3), axis=0)
    lam = jnp.sum(
        lax.dot_general(levels, onehot, (((1,), (1,)), ((), ())), preferred_element_type=jnp.float32),
        axis=0,
    )

    def tangents(direc):
        return lax.dot_general(
            direc, examples, (((1,), (1,)), ((), ())), preferred_element_type=jnp.float32
        )

    scaled = lam[None, :] * rhs
    sums = jnp.stack([jnp.sum(rhs * rhs, axis=1), jnp.sum(scaled * rhs, axis=1)])
    part = tangents(low)
    tang, sums = unpack(large_total(pack([part, sums], 8 * n_feat), "feat", 2), [part, sums])
    weighted = curvew[None, :] * tang
    sums = jnp.concatenate([sums, jnp.sum(weighted * tang, axis=1)[None, :]])
    (sums,) = unpack(small_total(pack([sums], 8), "ex", 3), [sums])
    norm_now, damp, along = sums[0], sums[1], sums[2]
    alpha = norm_now / (along / jnp.float32(total) + damp)

    prod = jnp.dot(weighted.astype(jnp.bfloat16), examples, preferred_element_type=jnp.float32)
    coef = jnp.broadcast_to((-alpha / jnp.float32(total))[:, None], (alpha.shape[0], LANES))
    resid, low = spread(prod, rhs - alpha[:, None] * scaled, coef, 4)

    stepped = lam[None, :] * resid
    sums = jnp.stack(
        [
            jnp.sum(resid * resid, axis=1),
            jnp.sum(stepped * resid, axis=1),
            jnp.sum(stepped * rhs, axis=1),
        ]
    )
    both = jnp.concatenate([rhs, resid]) * w_loc[None, :]
    pieces = jnp.concatenate(reduced(both, 2))
    rows = both.shape[0]
    grouped = jnp.dot(pieces, onehot, preferred_element_type=jnp.float32)
    grouped = grouped[:rows] + grouped[rows:]
    part = tangents(low)
    parts = [part, grouped, sums]
    turned, grouped, sums = unpack(large_total(pack(parts, 8 * n_feat), "feat", 5), parts)
    grouped = lax.dynamic_slice_in_dim(grouped, feat_pos * nb_feat, nb_feat, 1)
    heavy = curvew[None, :] * turned
    sums = jnp.concatenate(
        [sums, jnp.sum(heavy * turned, axis=1)[None, :], jnp.sum(heavy * tang, axis=1)[None, :]]
    )
    parts = [grouped, sums]
    grouped, sums = unpack(small_total(pack(parts, 8), "ex", 6), parts)
    norm_next = sums[0]
    beta = norm_next / norm_now
    curved = sums[3] + 2.0 * beta * sums[4] + beta * beta * along
    damped = sums[1] + 2.0 * beta * sums[2] + beta * beta * damp
    step = norm_next / (curved / jnp.float32(total) + damped)
    first = alpha + step * beta
    solve = first[:, None] * rhs + step[:, None] * resid
    grouped = lax.dynamic_slice_in_dim(grouped, ex_pos * nb_local, nb_local, 1)
    half = rows // 2
    block_sums = first[:, None] * grouped[:half] + step[:, None] * grouped[half:]
    own = lax.dynamic_slice_in_dim(
        strengths, (feat_pos * n_ex + ex_pos) * nb_local, nb_local, 0
    )
    return (solve, -own[None, :] * block_sums)


def solution(mesh):
    placed = (P("ex", "feat"), P("feat"), P("ex"), P("ex"), P(None, "ex"), P(), P("feat"))
    return jax.shard_map(
        shards,
        mesh=mesh,
        in_specs=placed,
        out_specs=(P(None, ("feat", "ex")), P(None, ("feat", "ex"))),
        check_vma=False,
    )
```

time: 696 us -> 289 us (0.42)
  waiting for transfers between devices: 282 us -> 0 us
  blocking collectives: 185 us -> 0 us
  Pallas kernels: 0 us -> 125 us
  matrix products: 186 us -> 140 us
  other arithmetic: 27.1 us -> 12.2 us
  between operations: 14.3 us -> 0.89 us
  local copies, waits for them, and re-layouts: 0.96 us -> 10 us
    psum x4 -> x0, blocking collectives: 143 us -> none  [the longest x2 80.4 us: norm_sum(): return lax.psum(jnp.sum(vec * vec, axis=1), ('feat', 'ex'))]
    psum x2 -> x0, waiting for transfers between devices: 141 us -> none  [shards(): tang = lax.psum(tang, 'feat')]
    pallas_call x0 -> x7, Pallas kernels: none -> 125 us  [the longest x2 72.4 us: spread(): pl.pallas_call(functools.partial(spread_kernel, n, share, based), out_sha...]
    reduce_scatter x3 -> x0, waiting for transfers between devices: 95.4 us -> none  [the longest x2 53.6 us: shards(): lax.psum_scatter(jnp.dot(wtang, examples, preferred_element_type=jnp.floa...]
    dot_general x8 -> x7, matrix products: 186 us -> 140 us  [the longest x2 58.2 us: tangents(): lax.dot_general(direc, examples, (((1,), (1,)), ((), ())), preferred_elem...]
    all_gather x2 -> x0, waiting for transfers between devices: 45.1 us -> none  [shards(): lax.all_gather(direc.astype(jnp.bfloat16), 'ex', axis=1, tiled=True)]
    unnamed x1 -> x0, blocking collectives: 42 us -> none
    eq x1 -> x0, other arithmetic: 15.8 us -> none  [shards(): block_ids[:, None] == jnp.arange(blocks, dtype=jnp.int32)[None, :]]
  transfers between devices with their start and end apart: 7 -> 0, of which waited for: 7 -> 0; matrix products, arithmetic and copies ran while one was open for 5% -> 0% of each run, Pallas kernels for 0% -> 0%
where the time goes in v1:
time: 289 us; the launch traced here: 288 us
  matrix products  140 us (48%)
  Pallas kernels  125 us (43%)
  other arithmetic  12.2 us (4%)
  local copies, waits for them, and re-layouts  10 us (3%)
    pallas_call x2, Pallas kernels, spread(): pl.pallas_call(functools.partial(spread_kernel, n, share, based), out_sha...  72.4 us
    dot_general x2, matrix products, tangents(): lax.dot_general(direc, examples, (((1,), (1,)), ((), ())), preferred_elem...  58.2 us
    pallas_call x2, Pallas kernels, large_total(): pl.pallas_call(functools.partial(reduce_kernel, axis, n), out_shape=jax.S...  33 us
    dot_general x1, matrix products, shards(): part = jnp.dot(examples, weights, preferred_element_type=jnp.float32)  27.3 us
    dot_general x1, matrix products, shards(): jnp.dot(gradw, examples, preferred_element_type=jnp.float32)  25.3 us
    dot_general x1, matrix products, shards(): jnp.dot(weighted.astype(jnp.bfloat16), examples, preferred_element_type=j...  25.3 us
    pallas_call x3, Pallas kernels, small_total(): pl.pallas_call(functools.partial(total_kernel, axis, n), out_shape=jax.Sh...  19.8 us

profile of v1, /device:TPU:0, one launch (start us, length us, event | category | flops | bytes accessed | tf_op | source)
XLA Modules:
  0.0 288.1 jit_solution(12744519559415890051)
XLA Ops:
  0.6 0.8 dynamic_slice.15
  1.4 0.7 reduce-precision_convert_fusion.2
  2.1 2.1 fusion.10
  4.2 0.9 reshape.196
  5.1 0.0 copy-start.3
  5.1 0.0 copy-start.4
  5.2 0.0 copy-start.2
  5.2 27.3 %fusion.46 = f32[1,1024]{1,0:T(1,128)} fusion(bf16[1024,32768]{1,0:T(8,128)(2,1)} %param.7, bf16[32768,1]{0,1:T(2,128)(2,1)S(1)} %reshape.196), kind=kOutput, calls=%fused_computation.101 | convolution fusion | flops 67108864 | bytes 67178496 | tf_op jit(solution)/shard_map/dot_general | solution.py:315
  32.4 9.8 %shard_map.86 = f32[8,128]{1,0:T(8,128)} custom-call(f32[8,128]{1,0:T(8,128)} %bitcast.133), custom_call_target="tpu_custom_call" | custom-call | tf_op jit(solution)/shard_map/pallas_call | solution.py:66
  42.2 0.0 copy-done.3
  42.2 0.0 copy-done.4
  42.2 0.7 fusion.27
  42.9 0.0 copy-done.2
  42.9 25.3 %fusion.18.refs_0_ = f32[32,32768]{1,0:T(8,128)} fusion(bf16[1024,32768]{1,0:T(8,128)(2,1)} %param.7, f32[32,1024]{1,0:T(8,128)S(1)} %copy-done.2, f32[1024]{0:T(1024)S(1)} %get-tuple-element.28), kind=kOutput, calls=%fused_computation.41 | convolution fusion | flops 2147581952 | bytes 71438336 | tf_op jit(solution)/shard_map/dot_general | solution.py:323
  68.2 35.5 %shard_map.87 = (f32[32,8192]{1,0:T(8,128)}, bf16[32,32768]{1,0:T(8,128)(2,1)}) custom-call(f32[32,32768]{1,0:T(8,128)} %fusion.18.refs_0_), custom_call_target="tpu_custom_call" | custom-call | tf_op jit(solution)/shard_map/pallas_call | solution.py:246
  103.7 1.5 multiply_reduce_fusion.1
  105.2 0.1 reshape.171
  105.3 0.0 copy-start
  105.3 29.1 %convolution_bitcast_fusion.1 = f32[4,8,8,128]{3,1,2,0:T(8,128)S(1)} fusion(bf16[32,32768]{1,0:T(8,128)(2,1)} %get-tuple-element.6, bf16[1024,32768]{1,0:T(8,128)(2,1)} %param.7), kind=kOutput, calls=%fused_computation.19 | convolution fusion | flops 2147483648 | bytes 69337088 | tf_op jit(solution)/shard_map/dot_general | solution.py:335
  134.5 0.7 select_maximum_fusion.2
  135.2 16.3 %shard_map.88 = f32[8,40,128]{2,1,0:T(8,128)} custom-call(f32[8,40,128]{2,1,0:T(8,128)} %bitcast.119), custom_call_target="tpu_custom_call" | custom-call | tf_op jit(solution)/shard_map/pallas_call | solution.py:125
  151.5 0.9 slice.104
  152.4 0.1 fusion.16
  152.5 0.7 slice_reduce_fusion.1
  153.2 0.1 reshape.175
  153.3 0.1 reshape.177
  153.4 0.6 pad.34.x_ref
  154.0 4.9 %shard_map.89 = f32[8,128]{1,0:T(8,128)} custom-call(f32[8,128]{1,0:T(8,128)} %pad.34.x_ref), custom_call_target="tpu_custom_call" | custom-call | tf_op jit(solution)/shard_map/pallas_call | solution.py:66
  158.9 0.9 negate_multiply_fusion
  159.8 0.0 copy-done
  159.8 1.2 fusion.9.refs_1_
  161.0 0.7 broadcast_in_dim.9.refs_2_
  161.6 25.3 %fusion.19.refs_0_ = f32[32,32768]{1,0:T(8,128)} fusion(bf16[1024,32768]{1,0:T(8,128)(2,1)} %param.7, f32[8,4,8,128]{3,2,1,0:T(8,128)S(1)} %bitcast.113, f32[1024]{0:T(1024)S(1)} %get-tuple-element.27), kind=kOutput, calls=%fused_computation.42 | convolution fusion | flops 2147549184 | bytes 71438336 | tf_op jit(solution)/shard_map/dot_general | solution.py:349
  186.9 36.9 %shard_map.90 = (f32[32,8192]{1,0:T(8,128)}, bf16[32,32768]{1,0:T(8,128)(2,1)}) custom-call(f32[32,32768]{1,0:T(8,128)} %fusion.19.refs_0_, f32[32,8192]{1,0:T(8,128)} %fusion.9.refs_1_, f32[32,128]{1,0:T(8,128)} %broadcast_in_dim.9.refs_2_), custom_call_target="tpu_custom_call" | custom-call | tf_op jit(solution)/shard_map/pallas_call | solution.py:246
  223.8 0.7 dynamic-slice_convert_fusion
  224.5 1.6 reduce-precision_convert_fusion
  226.1 1.6 fusion
  227.9 0.0 copy-start.1
  227.9 29.1 %convolution_bitcast_fusion = f32[4,8,8,128]{3,1,2,0:T(8,128)S(1)} fusion(bf16[32,32768]{1,0:T(8,128)(2,1)} %get-tuple-element.8, bf16[1024,32768]{1,0:T(8,128)(2,1)} %param.7), kind=kOutput, calls=%fused_computation.18 | convolution fusion | flops 2147483648 | bytes 69337088 | tf_op jit(solution)/shard_map/dot_general | solution.py:335
  257.0 0.0 copy-start.5
  257.1 0.0 copy-done.1
  257.1 0.4 fusion.12
  257.5 0.1 reshape.184
  257.6 0.7 select_maximum_fusion
  258.3 16.7 %shard_map.91 = f32[8,56,128]{2,1,0:T(8,128)} custom-call(f32[8,56,128]{2,1,0:T(8,128)} %bitcast.115), custom_call_target="tpu_custom_call" | custom-call | tf_op jit(solution)/shard_map/pallas_call | solution.py:125
  275.1 0.8 slice.107
  275.9 0.1 constant_dynamic-slice_fusion
  276.0 0.1 reshape.190
  276.1 0.9 slice.109
  277.0 0.1 fusion.14
  277.2 0.7 slice_reduce_fusion
  277.8 0.1 reshape.191
  277.9 0.1 reshape.193
  278.0 0.6 select_maximum_fusion.3.x_ref
  278.6 5.1 %shard_map.92 = f32[24,128]{1,0:T(8,128)} custom-call(f32[24,128]{1,0:T(8,128)} %select_maximum_fusion.3.x_ref), custom_call_target="tpu_custom_call" | custom-call | tf_op jit(solution)/shard_map/pallas_call | solution.py:66
  283.7 0.7 slice.100
  284.4 0.1 reshape_reshape.3
  284.5 0.7 slice_bitcast_fusion
  285.2 0.9 multiply_add_fusion.1
  286.0 0.0 copy-done.5
  286.0 0.1 dynamic-slice_negate_fusion
  286.1 0.1 fusion.25
  286.2 0.7 copy.25
  286.9 1.2 multiply_add_fusion
  (19 shorter events, 0.3 us)
Async XLA Ops:
  5.1 37.1 %copy-start.3 = (s32[1024]{0:T(1024)S(1)}, s32[1024]{0:T(1024)}, u32[]{:S(2)}) copy-start(s32[1024]{0:T(1024)} %param.10) | copy-start | bytes 12292
  5.1 37.1 %copy-start.4 = (s32[1024]{0:T(1024)S(1)}, s32[1024]{0:T(1024)}, u32[]{:S(2)}) copy-start(s32[1024]{0:T(1024)} %param.9) | copy-start | bytes 12292
  5.2 37.8 %copy-start.2 = (f32[32,1024]{1,0:T(8,128)S(1)}, f32[32,1024]{1,0:T(8,128)}, u32[]{:S(2)}) copy-start(f32[32,1024]{1,0:T(8,128)} %param.11) | copy-start | bytes 393220
  105.3 54.5 %copy-start = (f32[32,8192]{1,0:T(8,128)S(1)}, f32[32,8192]{1,0:T(8,128)}, u32[]{:S(2)}) copy-start(f32[32,8192]{1,0:T(8,128)} %get-tuple-element.7) | copy-start | bytes 3145732
  227.9 29.2 %copy-start.1 = (f32[32,8192]{1,0:T(8,128)S(1)}, f32[32,8192]{1,0:T(8,128)}, u32[]{:S(2)}) copy-start(f32[32,8192]{1,0:T(8,128)} %get-tuple-element.9) | copy-start | bytes 3145732
  257.0 29.0 %copy-start.5 = (f32[256]{0:T(256)S(1)}, f32[256]{0:T(256)}, u32[]{:S(2)}) copy-start(f32[256]{0:T(256)} %param.12) | copy-start | bytes 3076

commit v2 on v1

--- a/solution.py
+++ b/solution.py
@@ -138,18 +138,37 @@
     return out.reshape(rows, LANES)
 
 
-def spread_kernel(n, share, based, *refs):
+def spread_kernel(n, share, pieces, based, *refs):
     if based:
         x_ref, base_ref, coef_ref, own_ref, all_ref = refs[:5]
     else:
         x_ref, own_ref, all_ref = refs[:3]
-    acc, outbox, inbox, full, out_sem, in_sem, send_sem, recv_sem = refs[-8:]
+    scratch = refs[-8:]
     me = lax.axis_index("ex")
     masks = []
     while 2 ** len(masks) < n:
         masks.append(2 ** len(masks))
     meet("ex", [flip(me, mask) for mask in masks])
-
+    if based:
+        ends = (base_ref, coef_ref, own_ref, all_ref)
+    else:
+        ends = (None, None, own_ref, all_ref)
+    lanes = [
+        spread_piece(n, share, share // pieces, piece, masks, x_ref, ends, *[r.at[piece] for r in scratch])
+        for piece in range(pieces)
+    ]
+    while lanes:
+        lanes = [lane for lane in lanes if next(lane, None)]
+
+
+def spread_piece(n, share, size, piece, masks, x_ref, ends, acc, outbox, inbox, full, out_sem, in_sem, send_sem, recv_sem):
+    base_ref, coef_ref, own_ref, all_ref = ends
+    me = lax.axis_index("ex")
+
+    def columns(chunk):
+        return pl.ds(pl.multiple_of(chunk * share + piece * size, LANES), size)
+
+    here = pl.ds(piece * size, size)
     copies = []
     slot = 0
     for level, mask in enumerate(masks):
@@ -163,7 +182,7 @@
             away = group * 2 * mask + (1 - bit) * mask + low
             kept = group * 2 * mask + bit * mask + low
             if level == 0:
-                part = x_ref[:, pl.ds(pl.multiple_of(away * share, share), share)]
+                part = x_ref[:, columns(away)]
             else:
                 part = acc[away]
             outbox[slot] = part.astype(jnp.bfloat16)
@@ -178,10 +197,11 @@
             copy.start()
             sent.append((copy, kept, slot))
             slot += 1
+        yield True
         nexts = []
         for copy, kept, at in sent:
             if level == 0:
-                mine = x_ref[:, pl.ds(pl.multiple_of(kept * share, share), share)]
+                mine = x_ref[:, columns(kept)]
             else:
                 mine = acc[kept]
             nexts.append((copy, kept, at, mine))
@@ -189,10 +209,10 @@
             copy.wait_recv()
             acc[kept] = mine + inbox[at].astype(jnp.float32)
             copies.append(copy)
-    own = acc[me] if n > 1 else x_ref[...]
-    if based:
-        own = base_ref[...] + coef_ref[:, 0:1] * own
-    own_ref[...] = own
+    own = acc[me] if n > 1 else x_ref[:, here]
+    if base_ref is not None:
+        own = base_ref[:, here] + coef_ref[:, 0:1] * own
+    own_ref[:, here] = own
     full[me] = own.astype(jnp.bfloat16)
 
     ident = {}
@@ -220,8 +240,9 @@
     for mask in reversed(masks):
         live[mask, 0] = passing(mask, 0)
         live[mask, 0].start()
-    all_ref[:, pl.ds(pl.multiple_of(me * share, share), share)] = full[me]
+    all_ref[:, columns(me)] = full[me]
     for mask, offsets in order:
+        yield True
         for offset in offsets:
             live[mask, offset].wait_recv()
             arrived = mask ^ offset
@@ -230,7 +251,8 @@
                     live[smaller, arrived] = passing(smaller, arrived)
                     live[smaller, arrived].start()
             chunk = flip(me, arrived)
-            all_ref[:, pl.ds(pl.multiple_of(chunk * share, share), share)] = full[chunk]
+            all_ref[:, columns(chunk)] = full[chunk]
+    yield True
     for copy in copies:
         copy.wait_send()
     for copy in live.values():
@@ -243,8 +265,10 @@
     share = width // n
     based = base is not None
     count = max(n - 1, 1)
+    pieces = 4 if share % (4 * LANES) == 0 else 1
+    size = share // pieces
     return pl.pallas_call(
-        functools.partial(spread_kernel, n, share, based),
+        functools.partial(spread_kernel, n, share, pieces, based),
         out_shape=(
             jax.ShapeDtypeStruct((rows, share), jnp.float32),
             jax.ShapeDtypeStruct((rows, width), jnp.bfloat16),
@@ -252,12 +276,12 @@
         in_specs=[VMEM] * (3 if based else 1),
         out_specs=(VMEM, VMEM),
         scratch_shapes=[
-            pltpu.VMEM((n, rows, share), jnp.float32),
-            pltpu.VMEM((count, rows, share), jnp.bfloat16),
-            pltpu.VMEM((count, rows, share), jnp.bfloat16),
-            pltpu.VMEM((n, rows, share), jnp.bfloat16),
+            pltpu.VMEM((pieces, n, rows, size), jnp.float32),
+            pltpu.VMEM((pieces, count, rows, size), jnp.bfloat16),
+            pltpu.VMEM((pieces, count, rows, size), jnp.bfloat16),
+            pltpu.VMEM((pieces, n, rows, size), jnp.bfloat16),
         ]
-        + [pltpu.SemaphoreType.DMA((count,))] * 4,
+        + [pltpu.SemaphoreType.DMA((pieces, count))] * 4,
         compiler_params=pltpu.CompilerParams(collective_id=ident, has_side_effects=True),
     )(*((x, base, coef) if based else (x,)))
 

time: 289 us -> 282 us (0.976)
  Pallas kernels: 125 us -> 118 us
    pallas_call x2, Pallas kernels: 72.4 us -> 64.8 us  [spread(): pl.pallas_call(functools.partial(spread_kernel, n, share, pieces, based),...]
where the time goes in v2:
time: 282 us; the launch traced here: 280 us
  matrix products  140 us (50%)
  Pallas kernels  118 us (42%)
  other arithmetic  12.2 us (4%)
  local copies, waits for them, and re-layouts  10 us (4%)
    pallas_call x2, Pallas kernels, spread(): pl.pallas_call(functools.partial(spread_kernel, n, share, pieces, based),...  64.8 us
    dot_general x2, matrix products, tangents(): lax.dot_general(direc, examples, (((1,), (1,)), ((), ())), preferred_elem...  58.2 us
    pallas_call x2, Pallas kernels, large_total(): pl.pallas_call(functools.partial(reduce_kernel, axis, n), out_shape=jax.S...  33 us
    dot_general x1, matrix products, shards(): part = jnp.dot(examples, weights, preferred_element_type=jnp.float32)  27.3 us
    dot_general x1, matrix products, shards(): jnp.dot(gradw, examples, preferred_element_type=jnp.float32)  25.3 us
    dot_general x1, matrix products, shards(): jnp.dot(weighted.astype(jnp.bfloat16), examples, preferred_element_type=j...  25.2 us
    pallas_call x3, Pallas kernels, small_total(): pl.pallas_call(functools.partial(total_kernel, axis, n), out_shape=jax.Sh...  19.8 us

profile of v2, /device:TPU:0, one launch (start us, length us, event | category | flops | bytes accessed | tf_op | source)
XLA Modules:
  0.0 280.4 jit_solution(150778482704988172)
XLA Ops:
  0.6 0.8 dynamic_slice.15
  1.4 0.7 reduce-precision_convert_fusion.2
  2.1 2.1 fusion.10
  4.2 0.9 reshape.196
  5.1 0.0 copy-start.3
  5.1 0.0 copy-start.4
  5.2 0.0 copy-start.2
  5.2 27.3 %fusion.46 = f32[1,1024]{1,0:T(1,128)} fusion(bf16[1024,32768]{1,0:T(8,128)(2,1)} %param.7, bf16[32768,1]{0,1:T(2,128)(2,1)S(1)} %reshape.196), kind=kOutput, calls=%fused_computation.101 | convolution fusion | flops 67108864 | bytes 67178496 | tf_op jit(solution)/shard_map/dot_general | solution.py:339
  32.4 9.8 %shard_map.86 = f32[8,128]{1,0:T(8,128)} custom-call(f32[8,128]{1,0:T(8,128)} %bitcast.133), custom_call_target="tpu_custom_call" | custom-call | tf_op jit(solution)/shard_map/pallas_call | solution.py:66
  42.2 0.0 copy-done.3
  42.2 0.0 copy-done.4
  42.2 0.7 fusion.27
  42.9 0.0 copy-done.2
  42.9 25.3 %fusion.18.refs_0_ = f32[32,32768]{1,0:T(8,128)} fusion(bf16[1024,32768]{1,0:T(8,128)(2,1)} %param.7, f32[32,1024]{1,0:T(8,128)S(1)} %copy-done.2, f32[1024]{0:T(1024)S(1)} %get-tuple-element.28), kind=kOutput, calls=%fused_computation.41 | convolution fusion | flops 2147581952 | bytes 71438336 | tf_op jit(solution)/shard_map/dot_general | solution.py:347
  68.2 32.2 %shard_map.87 = (f32[32,8192]{1,0:T(8,128)}, bf16[32,32768]{1,0:T(8,128)(2,1)}) custom-call(f32[32,32768]{1,0:T(8,128)} %fusion.18.refs_0_), custom_call_target="tpu_custom_call" | custom-call | tf_op jit(solution)/shard_map/pallas_call | solution.py:270
  100.4 1.5 multiply_reduce_fusion.1
  101.9 0.1 reshape.171
  102.0 0.0 copy-start
  102.0 29.1 %convolution_bitcast_fusion.1 = f32[4,8,8,128]{3,1,2,0:T(8,128)S(1)} fusion(bf16[32,32768]{1,0:T(8,128)(2,1)} %get-tuple-element.6, bf16[1024,32768]{1,0:T(8,128)(2,1)} %param.7), kind=kOutput, calls=%fused_computation.19 | convolution fusion | flops 2147483648 | bytes 69337088 | tf_op jit(solution)/shard_map/dot_general | solution.py:359
  131.2 0.7 select_maximum_fusion.2
  131.9 16.3 %shard_map.88 = f32[8,40,128]{2,1,0:T(8,128)} custom-call(f32[8,40,128]{2,1,0:T(8,128)} %bitcast.119), custom_call_target="tpu_custom_call" | custom-call | tf_op jit(solution)/shard_map/pallas_call | solution.py:125
  148.2 0.9 slice.104
  149.1 0.1 fusion.16
  149.2 0.7 slice_reduce_fusion.1
  149.9 0.1 reshape.175
  150.0 0.1 reshape.177
  150.1 0.6 pad.34.x_ref
  150.7 4.9 %shard_map.89 = f32[8,128]{1,0:T(8,128)} custom-call(f32[8,128]{1,0:T(8,128)} %pad.34.x_ref), custom_call_target="tpu_custom_call" | custom-call | tf_op jit(solution)/shard_map/pallas_call | solution.py:66
  155.7 0.9 negate_multiply_fusion
  156.5 0.0 copy-done
  156.5 1.2 fusion.9.refs_1_
  157.7 0.7 broadcast_in_dim.9.refs_2_
  158.4 25.2 %fusion.19.refs_0_ = f32[32,32768]{1,0:T(8,128)} fusion(bf16[1024,32768]{1,0:T(8,128)(2,1)} %param.7, f32[8,4,8,128]{3,2,1,0:T(8,128)S(1)} %bitcast.113, f32[1024]{0:T(1024)S(1)} %get-tuple-element.27), kind=kOutput, calls=%fused_computation.42 | convolution fusion | flops 2147549184 | bytes 71438336 | tf_op jit(solution)/shard_map/dot_general | solution.py:373
  183.6 32.5 %shard_map.90 = (f32[32,8192]{1,0:T(8,128)}, bf16[32,32768]{1,0:T(8,128)(2,1)}) custom-call(f32[32,32768]{1,0:T(8,128)} %fusion.19.refs_0_, f32[32,8192]{1,0:T(8,128)} %fusion.9.refs_1_, f32[32,128]{1,0:T(8,128)} %broadcast_in_dim.9.refs_2_), custom_call_target="tpu_custom_call" | custom-call | tf_op jit(solution)/shard_map/pallas_call | solution.py:270
  216.2 0.7 dynamic-slice_convert_fusion
  216.9 1.6 reduce-precision_convert_fusion
  218.5 1.7 fusion
  220.2 0.0 copy-start.1
  220.2 29.1 %convolution_bitcast_fusion = f32[4,8,8,128]{3,1,2,0:T(8,128)S(1)} fusion(bf16[32,32768]{1,0:T(8,128)(2,1)} %get-tuple-element.8, bf16[1024,32768]{1,0:T(8,128)(2,1)} %param.7), kind=kOutput, calls=%fused_computation.18 | convolution fusion | flops 2147483648 | bytes 69337088 | tf_op jit(solution)/shard_map/dot_general | solution.py:359
  249.4 0.0 copy-start.5
  249.5 0.0 copy-done.1
  249.5 0.4 fusion.12
  249.9 0.1 reshape.184
  250.0 0.7 select_maximum_fusion
  250.7 16.7 %shard_map.91 = f32[8,56,128]{2,1,0:T(8,128)} custom-call(f32[8,56,128]{2,1,0:T(8,128)} %bitcast.115), custom_call_target="tpu_custom_call" | custom-call | tf_op jit(solution)/shard_map/pallas_call | solution.py:125
  267.4 0.8 slice.107
  268.3 0.1 constant_dynamic-slice_fusion
  268.4 0.1 reshape.190
  268.5 0.9 slice.109
  269.4 0.1 fusion.14
  269.5 0.7 slice_reduce_fusion
  270.2 0.1 reshape.191
  270.3 0.1 reshape.193
  270.4 0.6 select_maximum_fusion.3.x_ref
  271.0 5.1 %shard_map.92 = f32[24,128]{1,0:T(8,128)} custom-call(f32[24,128]{1,0:T(8,128)} %select_maximum_fusion.3.x_ref), custom_call_target="tpu_custom_call" | custom-call | tf_op jit(solution)/shard_map/pallas_call | solution.py:66
  276.1 0.7 slice.100
  276.8 0.1 reshape_reshape.3
  276.8 0.7 slice_bitcast_fusion
  277.5 0.9 multiply_add_fusion.1
  278.4 0.0 copy-done.5
  278.4 0.1 dynamic-slice_negate_fusion
  278.5 0.1 fusion.25
  278.6 0.7 copy.25
  279.2 1.2 multiply_add_fusion
  (19 shorter events, 0.3 us)
Async XLA Ops:
  5.1 37.1 %copy-start.3 = (s32[1024]{0:T(1024)S(1)}, s32[1024]{0:T(1024)}, u32[]{:S(2)}) copy-start(s32[1024]{0:T(1024)} %param.10) | copy-start | bytes 12292
  5.1 37.1 %copy-start.4 = (s32[1024]{0:T(1024)S(1)}, s32[1024]{0:T(1024)}, u32[]{:S(2)}) copy-start(s32[1024]{0:T(1024)} %param.9) | copy-start | bytes 12292
  5.2 37.8 %copy-start.2 = (f32[32,1024]{1,0:T(8,128)S(1)}, f32[32,1024]{1,0:T(8,128)}, u32[]{:S(2)}) copy-start(f32[32,1024]{1,0:T(8,128)} %param.11) | copy-start | bytes 393220
  102.0 54.5 %copy-start = (f32[32,8192]{1,0:T(8,128)S(1)}, f32[32,8192]{1,0:T(8,128)}, u32[]{:S(2)}) copy-start(f32[32,8192]{1,0:T(8,128)} %get-tuple-element.7) | copy-start | bytes 3145732
  220.2 29.2 %copy-start.1 = (f32[32,8192]{1,0:T(8,128)S(1)}, f32[32,8192]{1,0:T(8,128)}, u32[]{:S(2)}) copy-start(f32[32,8192]{1,0:T(8,128)} %get-tuple-element.9) | copy-start | bytes 3145732
  249.4 29.0 %copy-start.5 = (f32[256]{0:T(256)S(1)}, f32[256]{0:T(256)}, u32[]{:S(2)}) copy-start(f32[256]{0:T(256)} %param.12) | copy-start | bytes 3076
